TPU v7x, 32 devices: a whole 2x2x4 slice. The times are simulated.
32 devices in a mesh: wide: 8 (over z, x), narrow: 4 (over y, core).
Axes of the slice: x: 2, y: 2, z: 4, core: 2. Of those that a mesh axis runs over, the one named last changes fastest.
Arguments:
- states: bfloat16 [256, 262144], P('narrow', 'wide'), may hold values from -6 to 6
- obs_ens: bfloat16 [256, 32768], P('narrow', 'wide'), may hold values from -6 to 6
- obs_value: float32 [32768], P('wide'), may hold values from -6 to 6
- obs_prec: float32 [32768], P('wide'), may hold values from 0.1 to 1
- obs_pick: int32 [32, 1024], P('wide'), may hold values from 0 to 4607, as said below
- taper: float32 [32, 1024], P(('wide', 'narrow')), may hold values from 0.1 to 1
Outputs:
- analysis: bfloat16 [256, 262144], P('narrow', 'wide')
Inputs may be any that keep to these rules, and one draw needn't show every extreme that they name: `obs_pick`: within a region the 1024 rows are distinct.
All inputs are finite; a program needn't handle non-finite values.
Results may differ from a plain program's by a relative error of at most 0.0057.
Values may be sent and summed in bfloat16 or wider, within the bound.
No kernel may reach another device: no remote copies, remote signals or barrier semaphores. Data moves between devices by JAX's collectives and lax.ppermute only.
A program may use at most 64 MiB of HBM per device.

v0:
```python
import jax
import jax.numpy as jnp
from jax import lax
from jax.sharding import PartitionSpec as P

HALO = 256
ITERS = 6


def padded(array, sides, width):
    for axis, dim in sides:
        size, length = (lax.axis_size(axis), array.shape[dim])
        up = [(i, (i + 1) % size) for i in range(size)]
        down = [(j, i) for i, j in up]
        last = lax.slice_in_dim(array, length - width, length, axis=dim)
        leading = lax.slice_in_dim(array, 0, width, axis=dim)
        before = lax.ppermute(last, axis, up)
        after = lax.ppermute(leading, axis, down)
        array = jnp.concatenate([before, array, after], axis=dim)
    return array


def analyse(ensemble, observed, precision, taper_row, regional):
    members = ensemble.shape[0]
    obs_mean = jnp.mean(ensemble, axis=0)
    obs_pert = ensemble - obs_mean
    obs_weight = precision * taper_row
    scaled = (obs_pert * jnp.sqrt(obs_weight)).astype(jnp.bfloat16)
    identity = jnp.eye(members, dtype=jnp.float32)
    gram_sum = lax.dot_general(
        scaled, scaled, (((1,), (1,)), ((), ())), preferred_element_type=jnp.float32
    )
    precision_matrix = gram_sum + (members - 1.0) * identity
    forcing = jnp.dot(
        obs_pert,
        obs_weight * (observed - obs_mean),
        precision=lax.Precision.HIGHEST,
        preferred_element_type=jnp.float32,
    )
    norm_scale = jnp.sqrt(jnp.sum(precision_matrix * precision_matrix))
    current = precision_matrix / norm_scale
    root_iter = identity
    for iteration in range(ITERS):
        middle = 1.5 * identity - 0.5 * jnp.dot(
            root_iter, current, precision=lax.Precision.HIGHEST, preferred_element_type=jnp.float32
        )
        current = jnp.dot(
            current, middle, precision=lax.Precision.HIGHEST, preferred_element_type=jnp.float32
        )
        root_iter = jnp.dot(
            middle, root_iter, precision=lax.Precision.HIGHEST, preferred_element_type=jnp.float32
        )
    inv_root = root_iter / jnp.sqrt(norm_scale)
    inner = jnp.dot(
        inv_root, forcing, precision=lax.Precision.HIGHEST, preferred_element_type=jnp.float32
    )
    mean_weights = jnp.dot(
        inv_root, inner, precision=lax.Precision.HIGHEST, preferred_element_type=jnp.float32
    )
    transform = (jnp.sqrt(members - 1.0) * inv_root + mean_weights[:, None]).astype(jnp.bfloat16)
    state_mean = jnp.mean(regional.astype(jnp.float32), axis=0)
    state_pert = (regional.astype(jnp.float32) - state_mean).astype(jnp.bfloat16)
    mixed = lax.dot_general(
        transform, state_pert, (((0,), (0,)), ((), ())), preferred_element_type=jnp.float32
    )
    return (state_mean + mixed).astype(jnp.bfloat16)


def body(states, obs_ens, obs_value, obs_prec, obs_pick, taper):
    band_regions = lax.axis_size("narrow")
    position = lax.axis_index("narrow")
    members = obs_ens.shape[0] * band_regions
    extended = padded(obs_ens, (("wide", 1),), HALO)
    stat_pair = padded(jnp.stack([obs_value, obs_prec]), (("wide", 1),), HALO)
    own_rows = lax.dynamic_index_in_dim(obs_pick, position, 0, keepdims=False)
    chosen = jnp.take(extended, obs_pick.reshape(-1), axis=1).reshape(
        extended.shape[0], band_regions, -1
    )
    arrived = lax.all_to_all(chosen, "narrow", split_axis=1, concat_axis=0, tiled=True)
    picked = arrived.reshape(members, -1)
    stat_rows = jnp.take(stat_pair, own_rows, axis=1)
    regional = lax.all_to_all(states, "narrow", split_axis=1, concat_axis=0, tiled=True)
    result = analyse(picked.astype(jnp.float32), stat_rows[0], stat_rows[1], taper[0], regional)
    return lax.all_to_all(result, "narrow", split_axis=0, concat_axis=1, tiled=True)


def solution(mesh):
    return jax.shard_map(
        body,
        mesh=mesh,
        in_specs=(
            P("narrow", "wide"),
            P("narrow", "wide"),
            P("wide"),
            P("wide"),
            P("wide", None),
            P(("wide", "narrow"), None),
        ),
        out_specs=P("narrow", "wide"),
        check_vma=False,
    )
```

profile of v0, /device:TPU:0, one launch (start us, length us, event | category | flops | bytes accessed | tf_op | source)
XLA Modules:
  0.0 160.5 jit_solution(12780005530070920755)
XLA Ops:
  0.0 0.7 pad_maximum_fusion.3
  0.7 3.0 %collective-permute-start.2 = (f32[2,256]{1,0:T(2,128)S(1)}, f32[2,256]{1,0:T(2,128)S(1)}, u32[]{:S(2)}, u32[]{:S(2)}) collective-permute-start(f32[2,256]{1,0:T(2,128)S(1)} %get-tuple-element.11), channel_id=1, source_target_pairs={{0,4},{4,8},{8,12},{12,16},{16,20},{20,24},{24,28},{28,0},{1,5},{5... | collective-permute-start | bytes 6152 | tf_op jit(solution)/shard_map/ppermute | solution.py:17
  3.7 3.1 %collective-permute-start.3 = (f32[2,256]{1,0:T(2,128)S(1)}, f32[2,256]{1,0:T(2,128)S(1)}, u32[]{:S(2)}, u32[]{:S(2)}) collective-permute-start(f32[2,256]{1,0:T(2,128)S(1)} %get-tuple-element.12), channel_id=1, source_target_pairs={{4,0},{8,4},{12,8},{16,12},{20,16},{24,20},{28,24},{0,28},{5,1},{9... | collective-permute-start | bytes 6152 | tf_op jit(solution)/shard_map/ppermute | solution.py:18
  6.9 1.5 copy.24
  8.4 0.1 collective-permute-start
  8.5 4.7 %collective-permute-start.1 = (bf16[64,256]{0,1:T(8,128)(2,1)S(1)}, bf16[64,256]{0,1:T(8,128)(2,1)S(1)}, u32[]{:S(2)}, u32[]{:S(2)}) collective-permute-start(bf16[64,256]{0,1:T(8,128)(2,1)S(1)} %get-tuple-element.10), channel_id=1, source_target_pairs={{4,0},{8,4},{12,8},{16,12},{20,16},{24,20},{28,24},{0,28},{5,1},{9... | collective-permute-start | bytes 98312 | tf_op jit(solution)/shard_map/ppermute | solution.py:18
  13.2 0.7 compare_and_fusion
  13.9 0.7 compare_select_fusion.2
  14.7 0.7 copy.34
  15.4 0.9 copy.29
  16.4 4.6 %copy.36 = bf16[8,4,8,8192]{3,2,0,1:T(8,128)(2,1)} copy(bf16[8,4,8,8192]{3,2,1,0:T(8,128)(2,1)} %bitcast.95) | data formatting | bytes 8388608 | tf_op jit(solution)/shard_map/all_to_all | solution.py:82
  21.0 0.0 collective-permute-done
  21.0 0.0 collective-permute-done.1
  21.0 0.2 pad_maximum_fusion
  21.2 0.0 copy-start
  21.3 0.0 copy-start.1
  21.3 12.1 %gather_fusion = bf16[4096,64]{1,0:T(8,128)(2,1)S(1)} fusion(bf16[64,4608]{0,1:T(8,128)(2,1)S(1)} %pad_maximum_fusion, s32[4096]{0:T(1024)S(1)} %broadcast_clamp_fusion), kind=kCustom, calls=%fused_computation | custom fusion | bytes 1064960 | tf_op jit(solution)/shard_map/jit(_take)/gather | solution.py:76
  33.4 0.3 copy.27
  33.7 0.8 broadcast_select_fusion
  34.6 3.5 %all-to-all-start.1 = ((bf16[64,4,1024]{2,0,1:T(8,128)(2,1)}), bf16[64,4,1024]{2,0,1:T(8,128)(2,1)S(1)}, u32[]{:S(2)}, u32[]{:S(2)}) async-start(bf16[64,4,1024]{2,0,1:T(8,128)(2,1)} %broadcast_select_fusion), calls=%async_computation.1 | async-start | bytes 1048576 | tf_op jit(solution)/shard_map/all_to_all | solution.py:79
  38.1 0.0 collective-permute-done.2
  38.1 0.0 collective-permute-done.3
  38.1 0.0 copy-done
  38.1 0.0 copy-done.1
  38.1 0.7 copy.28
  38.9 4.0 %gather_fusion.1 = f32[1024,2]{1,0:T(8,128)} fusion(f32[2,4608]{0,1:T(8,128)S(1)} %copy.28, s32[1024]{0:T(1024)S(1)} %broadcast_clamp_fusion.1), kind=kCustom, calls=%fused_computation.1 | custom fusion | bytes 20480 | tf_op jit(solution)/shard_map/jit(_take)/gather | solution.py:81
  42.9 1.2 select_bitcast_fusion
  44.2 2.7 %all-to-all-done.1 = bf16[64,4,1024]{2,0,1:T(8,128)(2,1)S(1)} async-done(((bf16[64,4,1024]{2,0,1:T(8,128)(2,1)}), bf16[64,4,1024]{2,0,1:T(8,128)(2,1)S(1)}, u32[]{:S(2)}, u32[]{:S(2)}) %all-to-all-start.1) | async-done | bytes 524320 | tf_op jit(solution)/shard_map/all_to_all | solution.py:79
  46.8 5.0 %all-to-all-start = ((bf16[64,4,8192]{2,0,1:T(8,128)(2,1)}), bf16[64,4,8192]{2,0,1:T(8,128)(2,1)}, u32[]{:S(2)}, u32[]{:S(2)}) async-start(bf16[64,4,8192]{2,0,1:T(8,128)(2,1)} %bitcast.92), calls=%async_computation | async-start | bytes 8388608 | tf_op jit(solution)/shard_map/all_to_all | solution.py:82
  51.9 0.1 convert_reduce_fusion.1
  52.0 0.2 copy.30
  52.2 0.6 fusion.11
  52.8 0.1 fusion.9
  52.9 1.0 multiply_reduce_fusion
  54.6 0.3 fusion.7
  54.9 0.4 fusion.15
  55.3 0.3 fusion.12
  55.6 0.4 fusion.6
  56.0 0.4 fusion.19
  56.4 0.4 fusion.18
  56.8 0.4 fusion.5
  57.2 0.4 fusion.21
  57.5 0.4 fusion.20
  57.9 0.4 fusion.4
  58.3 0.4 fusion.23
  58.7 0.4 fusion.22
  59.1 0.4 fusion.3
  59.5 0.4 fusion.24
  59.9 0.4 fusion.25
  60.3 0.4 fusion.2
  60.6 0.4 convolution_divide_fusion
  61.0 0.1 fusion.8
  61.2 0.9 convolution_bitcast_fusion
  62.1 0.3 convolution_bitcast_fusion.1
  62.4 0.3 fusion.26
  62.7 37.2 %all-to-all-done = bf16[64,4,8192]{2,0,1:T(8,128)(2,1)} async-done(((bf16[64,4,8192]{2,0,1:T(8,128)(2,1)}), bf16[64,4,8192]{2,0,1:T(8,128)(2,1)}, u32[]{:S(2)}, u32[]{:S(2)}) %all-to-all-start) | async-done | bytes 4194336 | tf_op jit(solution)/shard_map/all_to_all | solution.py:82
  99.9 2.9 %convert_reduce_fusion = f32[8192]{0:T(1024)S(1)} fusion(bf16[64,4,8192]{2,0,1:T(8,128)(2,1)} %all-to-all-done), kind=kLoop, calls=%fused_computation.7 | loop fusion | flops 4186112 | bytes 4227072 | tf_op jit(solution)/shard_map/reduce_sum | solution.py:61
  102.8 3.3 %fusion.1 = bf16[256,8192]{1,0:T(8,128)(2,1)S(1)} fusion(f32[8192]{0:T(1024)S(1)} %broadcast_multiply_fusion, bf16[64,4,8192]{2,0,1:T(8,128)(2,1)} %all-to-all-done), kind=kLoop, calls=%fused_computation.5 | loop fusion | flops 6291456 | bytes 8421376 | tf_op jit(solution)/shard_map/convert_element_type | solution.py:62
  106.2 1.4 fusion
  107.5 50.7 %all_to_all.41 = bf16[4,64,8192]{2,1,0:T(8,128)(2,1)S(1)} all-to-all(bf16[4,64,8192]{2,1,0:T(8,128)(2,1)S(1)} %bitcast.91), channel_id=1, replica_groups=mesh['wide'=8,'narrow'=4] {'narrow'}, dimensions={0} | all-to-all | bytes 8388608 | tf_op jit(solution)/shard_map/all_to_all | solution.py:84
  158.2 2.3 %copy.33 = bf16[4,8,8,8192]{3,2,0,1:T(8,128)(2,1)} copy(bf16[4,8,8,8192]{3,2,1,0:T(8,128)(2,1)S(1)} %bitcast.93) | data formatting | bytes 8388608 | tf_op jit(solution)/shard_map/all_to_all | solution.py:84
  (8 shorter events, 0.1 us)
Async XLA Ops:
  0.7 37.3 %collective-permute-start.2 = (f32[2,256]{1,0:T(2,128)S(1)}, f32[2,256]{1,0:T(2,128)S(1)}, u32[]{:S(2)}, u32[]{:S(2)}) collective-permute-start(f32[2,256]{1,0:T(2,128)S(1)} %get-tuple-element.11), channel_id=1, source_target_pairs={{0,4},{4,8},{8,12},{12,16},{16,20},{20,24},{24,28},{28,0},{1,5},{5... | collective-permute-start | bytes 6152 | tf_op jit(solution)/shard_map/ppermute | solution.py:17
  3.7 34.3 %collective-permute-start.3 = (f32[2,256]{1,0:T(2,128)S(1)}, f32[2,256]{1,0:T(2,128)S(1)}, u32[]{:S(2)}, u32[]{:S(2)}) collective-permute-start(f32[2,256]{1,0:T(2,128)S(1)} %get-tuple-element.12), channel_id=1, source_target_pairs={{4,0},{8,4},{12,8},{16,12},{20,16},{24,20},{28,24},{0,28},{5,1},{9... | collective-permute-start | bytes 6152 | tf_op jit(solution)/shard_map/ppermute | solution.py:18
  8.4 12.6 %collective-permute-start = (bf16[64,256]{0,1:T(8,128)(2,1)S(1)}, bf16[64,256]{0,1:T(8,128)(2,1)S(1)}, u32[]{:S(2)}, u32[]{:S(2)}) collective-permute-start(bf16[64,256]{0,1:T(8,128)(2,1)S(1)} %get-tuple-element.9), channel_id=1, source_target_pairs={{0,4},{4,8},{8,12},{12,16},{16,20},{20,24},{24,28},{28,0},{1,5},{5... | collective-permute-start | bytes 98312 | tf_op jit(solution)/shard_map/ppermute | solution.py:17
  8.5 12.5 %collective-permute-start.1 = (bf16[64,256]{0,1:T(8,128)(2,1)S(1)}, bf16[64,256]{0,1:T(8,128)(2,1)S(1)}, u32[]{:S(2)}, u32[]{:S(2)}) collective-permute-start(bf16[64,256]{0,1:T(8,128)(2,1)S(1)} %get-tuple-element.10), channel_id=1, source_target_pairs={{4,0},{8,4},{12,8},{16,12},{20,16},{24,20},{28,24},{0,28},{5,1},{9... | collective-permute-start | bytes 98312 | tf_op jit(solution)/shard_map/ppermute | solution.py:18
  21.2 16.8 %copy-start = (f32[4096]{0:T(1024)S(1)}, f32[4096]{0:T(1024)}, u32[]{:S(2)}) copy-start(f32[4096]{0:T(1024)} %param.9) | copy-start | bytes 49156
  21.3 16.8 %copy-start.1 = (f32[4096]{0:T(1024)S(1)}, f32[4096]{0:T(1024)}, u32[]{:S(2)}) copy-start(f32[4096]{0:T(1024)} %param.8) | copy-start | bytes 49156
  34.6 12.3 %all-to-all-start.1 = ((bf16[64,4,1024]{2,0,1:T(8,128)(2,1)}), bf16[64,4,1024]{2,0,1:T(8,128)(2,1)S(1)}, u32[]{:S(2)}, u32[]{:S(2)}) async-start(bf16[64,4,1024]{2,0,1:T(8,128)(2,1)} %broadcast_select_fusion), calls=%async_computation.1 | async-start | bytes 1048576 | tf_op jit(solution)/shard_map/all_to_all | solution.py:79
  46.8 53.1 %all-to-all-start = ((bf16[64,4,8192]{2,0,1:T(8,128)(2,1)}), bf16[64,4,8192]{2,0,1:T(8,128)(2,1)}, u32[]{:S(2)}, u32[]{:S(2)}) async-start(bf16[64,4,8192]{2,0,1:T(8,128)(2,1)} %bitcast.92), calls=%async_computation | async-start | bytes 8388608 | tf_op jit(solution)/shard_map/all_to_all | solution.py:82
where the time goes:
time: 161 us
  blocking collectives  50.7 us (31%)
  waiting for transfers between devices  39.9 us (25%)
  local copies, waits for them, and re-layouts  27.6 us (17%)
  starting transfers between devices  19.4 us (12%)
  other arithmetic  11.7 us (7%)
  matrix products  10.2 us (6%)
    all_to_all x1, blocking collectives, body(): lax.all_to_all(result, 'narrow', split_axis=0, concat_axis=1, tiled=True)  50.7 us
    all_to_all x1, waiting for transfers between devices, body(): lax.all_to_all(states, 'narrow', split_axis=1, concat_axis=0, tiled=True)  37.2 us
    gather x2, local copies, waits for them, and re-layouts, body(): jnp.take(extended, obs_pick.reshape(-1), axis=1)  12.5 us
    ppermute x2, starting transfers between devices, padded(): after = lax.ppermute(leading, axis, down)  7.81 us
    all_to_all x1, starting transfers between devices, body(): lax.all_to_all(states, 'narrow', split_axis=1, concat_axis=0, tiled=True)  5.04 us
    all_to_all x1, local copies, waits for them, and re-layouts, body(): lax.all_to_all(states, 'narrow', split_axis=1, concat_axis=0, tiled=True)  4.64 us
    gather x1, local copies, waits for them, and re-layouts, body(): stat_rows = jnp.take(stat_pair, own_rows, axis=1)  4.04 us
    all_to_all x1, starting transfers between devices, body(): lax.all_to_all(chosen, 'narrow', split_axis=1, concat_axis=0, tiled=True)  3.47 us
  transfers between devices with their start and end apart: 6, of which 2 were waited for; matrix products, arithmetic and copies ran while one was open for 24% of the time, Pallas kernels for 0%

commit v1 on v0

--- a/solution.py
+++ b/solution.py
@@ -5,6 +5,28 @@
 
 HALO = 256
 ITERS = 6
+
+
+def in_blocks(array, dim, size):
+    before, after = (array.shape[:dim], array.shape[dim + 1 :])
+    return jnp.moveaxis(array.reshape(*before, size, -1, *after), dim, 0)
+
+
+def in_order(pieces, dim):
+    pieces = jnp.moveaxis(pieces, 0, dim)
+    lengths = pieces.shape
+    return pieces.reshape(*lengths[:dim], lengths[dim] * lengths[dim + 1], *lengths[dim + 2 :])
+
+
+def rotated_exchange(shard, axis, split_dim, concat_dim):
+    devices, index = (lax.axis_size(axis), lax.axis_index(axis))
+    parts = in_blocks(shard, split_dim, devices)
+    done = [parts[index]]
+    for step in range(1, devices):
+        sent = parts[(index + step) % devices]
+        done.append(lax.ppermute(sent, axis, [(i, (i + step) % devices) for i in range(devices)]))
+    parts = jnp.stack(done)[(index - jnp.arange(devices)) % devices]
+    return in_order(parts, concat_dim)
 
 
 def padded(array, sides, width):
@@ -79,7 +101,7 @@
     arrived = lax.all_to_all(chosen, "narrow", split_axis=1, concat_axis=0, tiled=True)
     picked = arrived.reshape(members, -1)
     stat_rows = jnp.take(stat_pair, own_rows, axis=1)
-    regional = lax.all_to_all(states, "narrow", split_axis=1, concat_axis=0, tiled=True)
+    regional = rotated_exchange(states, "narrow", 1, 0)
     result = analyse(picked.astype(jnp.float32), stat_rows[0], stat_rows[1], taper[0], regional)
     return lax.all_to_all(result, "narrow", split_axis=0, concat_axis=1, tiled=True)
 

time: 161 us -> 158 us (0.981)
  local copies, waits for them, and re-layouts: 27.6 us -> 58.9 us
  waiting for transfers between devices: 39.9 us -> 9 us
  starting transfers between devices: 19.4 us -> 16.2 us
    all_to_all x1 -> x0, waiting for transfers between devices: 37.2 us -> none  [body(): lax.all_to_all(states, 'narrow', split_axis=1, concat_axis=0, tiled=True)]
    another operation x0 -> x1, local copies, waits for them, and re-layouts: none -> 15 us
    unnamed x7 -> x21, local copies, waits for them, and re-layouts: 3.17 us -> 11.5 us
    reshape x0 -> x1, local copies, waits for them, and re-layouts: none -> 7.83 us  [in_blocks(): return jnp.moveaxis(array.reshape(*before, size, -1, *after), dim, 0)]
    all_to_all x1, waiting for transfers between devices: 2.69 us -> 8.93 us  [body(): lax.all_to_all(chosen, 'narrow', split_axis=1, concat_axis=0, tiled=True)]
    all_to_all x1 -> x0, starting transfers between devices: 5.04 us -> none  [body(): lax.all_to_all(states, 'narrow', split_axis=1, concat_axis=0, tiled=True)]
    gather x0 -> x1, local copies, waits for them, and re-layouts: none -> 4.94 us  [rotated_exchange(): parts = jnp.stack(done)[(index - jnp.arange(devices)) % devices]]
    all_to_all x1 -> x0, local copies, waits for them, and re-layouts: 4.64 us -> none  [body(): lax.all_to_all(states, 'narrow', split_axis=1, concat_axis=0, tiled=True)]
  transfers between devices with their start and end apart: 6 -> 8, of which waited for: 2 -> 2; matrix products, arithmetic and copies ran while one was open for 24% -> 24% of each run, Pallas kernels for 0% -> 0%
where the time goes in v1:
time: 158 us
  local copies, waits for them, and re-layouts  58.9 us (37%)
  blocking collectives  51.5 us (33%)
  starting transfers between devices  16.2 us (10%)
  other arithmetic  11 us (7%)
  matrix products  10.1 us (6%)
  waiting for transfers between devices  9 us (6%)
    all_to_all x1, blocking collectives, body(): lax.all_to_all(result, 'narrow', split_axis=0, concat_axis=1, tiled=True)  51.5 us
    another operation x1, local copies, waits for them, and re-layouts  15 us
    gather x2, local copies, waits for them, and re-layouts, body(): jnp.take(extended, obs_pick.reshape(-1), axis=1)  12.5 us
    unnamed x21, local copies, waits for them, and re-layouts  11.5 us
    ppermute x2, starting transfers between devices, padded(): after = lax.ppermute(leading, axis, down)  9.3 us
    all_to_all x1, waiting for transfers between devices, body(): lax.all_to_all(chosen, 'narrow', split_axis=1, concat_axis=0, tiled=True)  8.93 us
    reshape x1, local copies, waits for them, and re-layouts, in_blocks(): return jnp.moveaxis(array.reshape(*before, size, -1, *after), dim, 0)  7.83 us
    gather x1, local copies, waits for them, and re-layouts, rotated_exchange(): parts = jnp.stack(done)[(index - jnp.arange(devices)) % devices]  4.94 us
  transfers between devices with their start and end apart: 8, of which 2 were waited for; matrix products, arithmetic and copies ran while one was open for 24% of the time, Pallas kernels for 0%

profile of v1, /device:TPU:0, one launch (start us, length us, event | category | flops | bytes accessed | tf_op | source)
XLA Modules:
  0.0 157.8 jit_solution(15635196586319729200)
XLA Ops:
  0.0 7.8 %reshape.193 = bf16[64,4,8192]{2,1,0:T(4,128)(2,1)} reshape(bf16[64,32768]{1,0:T(8,128)(2,1)} %param.6) | data formatting | bytes 8388608 | tf_op jit(solution)/shard_map/reshape | solution.py:12
  7.8 15.0 %constant_dynamic-slice_fusion.4 = (bf16[64,1,8192]{2,1,0:T(2,128)(2,1)S(1)}, bf16[64,1,8192]{2,1,0:T(2,128)(2,1)S(1)}, bf16[64,1,8192]{2,1,0:T(2,128)(2,1)S(1)}, bf16[64,1,8192]{2,1,0:T(2,128)(2,1)S(1)}) fusion(bf16[64,4,8192]{2,1,0:T(4,128)(2,1)} %reshape.193, s32[]{:T(128)S(6)} %select_n.94, s32[]{:T(128)S(6)} %select_n.100, s32[]{:T(128)S(6)} %select_n.98, ...), kind=kLoop, calls=%fused_computation.72 | loop fusion | bytes 8388624 | tf_op jit(solution)/shard_map/dynamic-slice
  22.8 2.1 %copy.48 = bf16[64,1,8192]{2,0,1:T(8,128)(2,1)} copy(bf16[64,1,8192]{2,1,0:T(2,128)(2,1)S(1)} %get-tuple-element.10) | data formatting | bytes 2097152
  24.9 2.4 %collective-permute-start.2 = (bf16[64,8192]{1,0:T(8,128)(2,1)}, bf16[64,8192]{1,0:T(8,128)(2,1)}, u32[]{:S(2)}, u32[]{:S(2)}) collective-permute-start(bf16[64,8192]{1,0:T(8,128)(2,1)} %bitcast.98), channel_id=1, source_target_pairs={{0,3},{1,0},{2,1},{3,2},{4,7},{5,4},{6,5},{7,6},{8,11},{9,8},{10,9... | collective-permute-start | bytes 3145736 | tf_op jit(solution)/shard_map/ppermute | solution.py:27
  27.4 2.1 %copy.49 = bf16[64,1,8192]{2,0,1:T(8,128)(2,1)} copy(bf16[64,1,8192]{2,1,0:T(2,128)(2,1)S(1)} %get-tuple-element.11) | data formatting | bytes 2097152
  29.5 0.6 collective-permute-start.1
  30.0 2.1 %copy.50 = bf16[64,1,8192]{2,0,1:T(8,128)(2,1)} copy(bf16[64,1,8192]{2,1,0:T(2,128)(2,1)S(1)} %get-tuple-element.12) | data formatting | bytes 2097152
  32.2 0.2 collective-permute-start
  32.4 1.5 copy.30
  33.9 4.6 %collective-permute-start.4 = (bf16[64,256]{0,1:T(8,128)(2,1)S(1)}, bf16[64,256]{0,1:T(8,128)(2,1)S(1)}, u32[]{:S(2)}, u32[]{:S(2)}) collective-permute-start(bf16[64,256]{0,1:T(8,128)(2,1)S(1)} %get-tuple-element.14), channel_id=1, source_target_pairs={{4,0},{8,4},{12,8},{16,12},{20,16},{24,20},{28,24},{0,28},{5,1},{9... | collective-permute-start | bytes 98312 | tf_op jit(solution)/shard_map/ppermute | solution.py:40
  38.5 0.0 collective-permute-start.3
  38.7 2.1 %copy.51 = bf16[64,1,8192]{2,0,1:T(8,128)(2,1)} copy(bf16[64,1,8192]{2,1,0:T(2,128)(2,1)S(1)} %get-tuple-element.9) | data formatting | bytes 2097152
  40.9 1.0 copy.35
  41.9 0.0 collective-permute-done.4
  41.9 4.7 %collective-permute-start.6 = (f32[2,256]{1,0:T(2,128)S(1)}, f32[2,256]{1,0:T(2,128)S(1)}, u32[]{:S(2)}, u32[]{:S(2)}) collective-permute-start(f32[2,256]{1,0:T(2,128)S(1)} %get-tuple-element.16), channel_id=1, source_target_pairs={{4,0},{8,4},{12,8},{16,12},{20,16},{24,20},{28,24},{0,28},{5,1},{9... | collective-permute-start | bytes 6152 | tf_op jit(solution)/shard_map/ppermute | solution.py:40
  46.6 0.0 collective-permute-done.3
  46.6 0.0 collective-permute-start.5
  46.6 0.2 pad_maximum_fusion.1
  46.9 12.1 %gather_fusion.1 = bf16[4096,64]{1,0:T(8,128)(2,1)S(1)} fusion(bf16[64,4608]{0,1:T(8,128)(2,1)S(1)} %pad_maximum_fusion.1, s32[4096]{0:T(1024)S(1)} %broadcast_clamp_fusion), kind=kCustom, calls=%fused_computation.1 | custom fusion | bytes 1064960 | tf_op jit(solution)/shard_map/jit(_take)/gather | solution.py:98
  59.0 0.3 copy.33
  59.4 0.9 broadcast_select_fusion
  60.2 3.6 %all-to-all-start = ((bf16[64,4,1024]{2,0,1:T(8,128)(2,1)}), bf16[64,4,1024]{2,0,1:T(8,128)(2,1)S(1)}, u32[]{:S(2)}, u32[]{:S(2)}) async-start(bf16[64,4,1024]{2,0,1:T(8,128)(2,1)} %broadcast_select_fusion), calls=%async_computation | async-start | bytes 1048576 | tf_op jit(solution)/shard_map/all_to_all | solution.py:101
  63.9 0.0 collective-permute-done.6
  63.9 0.0 collective-permute-done.5
  63.9 0.7 copy.34
  64.7 4.0 %gather_fusion.2 = f32[1024,2]{1,0:T(8,128)} fusion(f32[2,4608]{0,1:T(8,128)S(1)} %copy.34, s32[1024]{0:T(1024)S(1)} %broadcast_clamp_fusion.1), kind=kCustom, calls=%fused_computation.2 | custom fusion | bytes 20480 | tf_op jit(solution)/shard_map/jit(_take)/gather | solution.py:103
  68.6 1.2 select_bitcast_fusion
  69.9 8.9 %all-to-all-done = bf16[64,4,1024]{2,0,1:T(8,128)(2,1)S(1)} async-done(((bf16[64,4,1024]{2,0,1:T(8,128)(2,1)}), bf16[64,4,1024]{2,0,1:T(8,128)(2,1)S(1)}, u32[]{:S(2)}, u32[]{:S(2)}) %all-to-all-start) | async-done | bytes 524320 | tf_op jit(solution)/shard_map/all_to_all | solution.py:101
  78.8 0.1 convert_reduce_fusion.1
  78.9 0.2 copy.36
  79.2 0.6 fusion.11
  79.7 0.1 fusion.9
  79.9 0.9 multiply_reduce_fusion
  81.4 0.3 fusion.7
  81.7 0.3 fusion.12
  82.0 0.4 fusion.15
  82.4 0.4 fusion.6
  82.8 0.4 fusion.20
  83.1 0.4 fusion.21
  83.5 0.4 fusion.5
  83.9 0.4 fusion.22
  84.3 0.4 fusion.23
  84.7 0.4 fusion.4
  85.1 0.4 fusion.24
  85.5 0.4 fusion.25
  85.9 0.4 fusion.3
  86.3 0.4 fusion.26
  86.6 0.4 fusion.27
  87.1 0.4 fusion.2
  87.5 0.4 convolution_divide_fusion
  87.8 0.1 fusion.8
  88.0 0.9 convolution_bitcast_fusion
  88.9 0.3 convolution_bitcast_fusion.1
  89.2 0.3 fusion.28
  89.5 0.1 collective-permute-done.1
  89.6 0.0 collective-permute-done
  89.6 3.6 %pad_maximum_fusion = bf16[4,64,8192]{2,1,0:T(8,128)(2,1)} fusion(bf16[1,64,8192]{2,1,0:T(8,128)(2,1)} %bitcast.2, bf16[1,64,8192]{2,1,0:T(8,128)(2,1)} %bitcast.1, bf16[1,64,8192]{2,1,0:T(8,128)(2,1)} %bitcast, bf16[1,64,8192]{2,1,0:T(8,128)(2,1)S(1)} %bitcast.105), kind=kLoop, calls=%fused_computation.7 | loop fusion | flops 6291456 | bytes 8388608 | tf_op jit(solution)/shard_map/stack | solution.py:28
  93.2 4.9 %gather_fusion = bf16[4,64,8192]{2,1,0:T(8,128)(2,1)} fusion(bf16[4,64,8192]{2,1,0:T(8,128)(2,1)} %pad_maximum_fusion, s32[1024]{0:T(1024)S(1)} %pad_clamp_fusion), kind=kCustom, calls=%fused_computation | custom fusion | bytes 8388624 | tf_op jit(solution)/shard_map/gather | solution.py:28
  98.2 3.0 %convert_reduce_fusion = f32[8192]{0:T(1024)S(1)} fusion(bf16[4,64,8192]{2,1,0:T(8,128)(2,1)} %gather_fusion), kind=kLoop, calls=%fused_computation.8 | loop fusion | flops 4186112 | bytes 4227072 | tf_op jit(solution)/shard_map/reduce_sum | solution.py:83
  101.2 0.4 copy-done
  101.6 0.9 fusion.1
  102.6 1.4 fusion
  104.0 51.5 %all_to_all.28 = bf16[4,64,8192]{2,1,0:T(8,128)(2,1)S(1)} all-to-all(bf16[4,64,8192]{2,1,0:T(8,128)(2,1)S(1)} %bitcast.102), channel_id=1, replica_groups=mesh['wide'=8,'narrow'=4] {'narrow'}, dimensions={0} | all-to-all | bytes 8388608 | tf_op jit(solution)/shard_map/all_to_all | solution.py:106
  155.5 2.3 %copy.42 = bf16[4,8,8,8192]{3,2,0,1:T(8,128)(2,1)} copy(bf16[4,8,8,8192]{3,2,1,0:T(8,128)(2,1)S(1)} %bitcast.103) | data formatting | bytes 8388608 | tf_op jit(solution)/shard_map/all_to_all | solution.py:106
  (28 shorter events, 0.2 us)
Async XLA Ops:
  24.9 13.6 %copy-start.3 = (s32[4,1024]{1,0:T(4,128)S(1)}, s32[4,1024]{1,0:T(4,128)}, u32[]{:S(2)}) copy-start(s32[4,1024]{1,0:T(4,128)} %param.10) | copy-start | bytes 49156
  24.9 13.8 %copy-start.4 = (f32[4096]{0:T(1024)S(1)}, f32[4096]{0:T(1024)}, u32[]{:S(2)}) copy-start(f32[4096]{0:T(1024)} %param.9) | copy-start | bytes 49156
  24.9 13.8 %copy-start.5 = (f32[4096]{0:T(1024)S(1)}, f32[4096]{0:T(1024)}, u32[]{:S(2)}) copy-start(f32[4096]{0:T(1024)} %param.8) | copy-start | bytes 49156
  24.9 64.6 %collective-permute-start.2 = (bf16[64,8192]{1,0:T(8,128)(2,1)}, bf16[64,8192]{1,0:T(8,128)(2,1)}, u32[]{:S(2)}, u32[]{:S(2)}) collective-permute-start(bf16[64,8192]{1,0:T(8,128)(2,1)} %bitcast.98), channel_id=1, source_target_pairs={{0,3},{1,0},{2,1},{3,2},{4,7},{5,4},{6,5},{7,6},{8,11},{9,8},{10,9... | collective-permute-start | bytes 3145736 | tf_op jit(solution)/shard_map/ppermute | solution.py:27
  29.5 11.4 %copy-start.6 = (f32[1,1024]{1,0:T(1,128)S(1)}, f32[1,1024]{1,0:T(1,128)}, u32[]{:S(2)}) copy-start(f32[1,1024]{1,0:T(1,128)} %param.11) | copy-start | bytes 12292
  29.5 60.1 %collective-permute-start.1 = (bf16[64,8192]{1,0:T(8,128)(2,1)}, bf16[64,8192]{1,0:T(8,128)(2,1)}, u32[]{:S(2)}, u32[]{:S(2)}) collective-permute-start(bf16[64,8192]{1,0:T(8,128)(2,1)} %bitcast.99), channel_id=1, source_target_pairs={{0,2},{1,3},{2,0},{3,1},{4,6},{5,7},{6,4},{7,5},{8,10},{9,11},{10,... | collective-permute-start | bytes 3145736 | tf_op jit(solution)/shard_map/ppermute | solution.py:27
  32.2 57.4 %collective-permute-start = (bf16[64,8192]{1,0:T(8,128)(2,1)}, bf16[64,8192]{1,0:T(8,128)(2,1)}, u32[]{:S(2)}, u32[]{:S(2)}) collective-permute-start(bf16[64,8192]{1,0:T(8,128)(2,1)} %bitcast.100), channel_id=1, source_target_pairs={{0,1},{1,2},{2,3},{3,0},{4,5},{5,6},{6,7},{7,4},{8,9},{9,10},{10,1... | collective-permute-start | bytes 3145736 | tf_op jit(solution)/shard_map/ppermute | solution.py:27
  33.9 8.0 %collective-permute-start.4 = (bf16[64,256]{0,1:T(8,128)(2,1)S(1)}, bf16[64,256]{0,1:T(8,128)(2,1)S(1)}, u32[]{:S(2)}, u32[]{:S(2)}) collective-permute-start(bf16[64,256]{0,1:T(8,128)(2,1)S(1)} %get-tuple-element.14), channel_id=1, source_target_pairs={{4,0},{8,4},{12,8},{16,12},{20,16},{24,20},{28,24},{0,28},{5,1},{9... | collective-permute-start | bytes 98312 | tf_op jit(solution)/shard_map/ppermute | solution.py:40
  38.5 8.1 %collective-permute-start.3 = (bf16[64,256]{0,1:T(8,128)(2,1)S(1)}, bf16[64,256]{0,1:T(8,128)(2,1)S(1)}, u32[]{:S(2)}, u32[]{:S(2)}) collective-permute-start(bf16[64,256]{0,1:T(8,128)(2,1)S(1)} %get-tuple-element.13), channel_id=1, source_target_pairs={{0,4},{4,8},{8,12},{12,16},{16,20},{20,24},{24,28},{28,0},{1,5},{5... | collective-permute-start | bytes 98312 | tf_op jit(solution)/shard_map/ppermute | solution.py:39
  41.9 22.0 %collective-permute-start.6 = (f32[2,256]{1,0:T(2,128)S(1)}, f32[2,256]{1,0:T(2,128)S(1)}, u32[]{:S(2)}, u32[]{:S(2)}) collective-permute-start(f32[2,256]{1,0:T(2,128)S(1)} %get-tuple-element.16), channel_id=1, source_target_pairs={{4,0},{8,4},{12,8},{16,12},{20,16},{24,20},{28,24},{0,28},{5,1},{9... | collective-permute-start | bytes 6152 | tf_op jit(solution)/shard_map/ppermute | solution.py:40
  46.6 17.3 %collective-permute-start.5 = (f32[2,256]{1,0:T(2,128)S(1)}, f32[2,256]{1,0:T(2,128)S(1)}, u32[]{:S(2)}, u32[]{:S(2)}) collective-permute-start(f32[2,256]{1,0:T(2,128)S(1)} %get-tuple-element.15), channel_id=1, source_target_pairs={{0,4},{4,8},{8,12},{12,16},{16,20},{20,24},{24,28},{28,0},{1,5},{5... | collective-permute-start | bytes 6152 | tf_op jit(solution)/shard_map/ppermute | solution.py:39
  59.0 20.1 %copy-start.2 = (f32[1,1024]{0,1:T(8,128)S(1)}, f32[1,1024]{0,1:T(8,128)}, u32[]{:S(2)}) copy-start(f32[1,1024]{0,1:T(8,128)} %copy.35) | copy-start | bytes 12292
  60.2 18.6 %all-to-all-start = ((bf16[64,4,1024]{2,0,1:T(8,128)(2,1)}), bf16[64,4,1024]{2,0,1:T(8,128)(2,1)S(1)}, u32[]{:S(2)}, u32[]{:S(2)}) async-start(bf16[64,4,1024]{2,0,1:T(8,128)(2,1)} %broadcast_select_fusion), calls=%async_computation | async-start | bytes 1048576 | tf_op jit(solution)/shard_map/all_to_all | solution.py:101
  85.5 4.1 %copy-start.1 = (bf16[64,1,8192]{2,0,1:T(8,128)(2,1)S(1)}, bf16[64,1,8192]{2,0,1:T(8,128)(2,1)}, u32[]{:S(2)}) copy-start(bf16[64,1,8192]{2,0,1:T(8,128)(2,1)} %copy.51) | copy-start | bytes 3145732
  98.2 3.4 %copy-start = (bf16[4,64,8192]{2,1,0:T(8,128)(2,1)S(1)}, bf16[4,64,8192]{2,1,0:T(8,128)(2,1)}, u32[]{:S(2)}) copy-start(bf16[4,64,8192]{2,1,0:T(8,128)(2,1)} %gather_fusion) | copy-start | bytes 12582916
